TPU v7x, 32 devices: a whole 2x2x4 slice. The times are simulated.
32 devices in a mesh: dp: 4 (over y, x), fsdp: 4 (over z), ctx: 2 (over core).
Axes of the slice: x: 2, y: 2, z: 4, core: 2. Of those that a mesh axis runs over, the one named last changes fastest.
Arguments:
- inputs: bfloat16 [16, 1024, 1024], P(('dp', 'fsdp'), 'ctx'), may hold values from -6 to 6
- lengths: int32 [16], P(('dp', 'fsdp')), may hold values from 256 to 1024, as said below
- cotangent: bfloat16 [16, 1024, 1024], P(('dp', 'fsdp'), 'ctx'), may hold values from -6 to 6
- norm_gain1: float32 [1024], replicated, may hold values from 0.5 to 1.5
- w_qkv: bfloat16 [1024, 3072], P('fsdp'), may hold values from -0.1875 to 0.1875
- w_beta: bfloat16 [1024, 8], P('fsdp'), may hold values from -0.1875 to 0.1875
- conv_weight: float32 [4, 3072], replicated, may hold values from -3 to 3
- head_gain: float32 [128], replicated, may hold values from 0.5 to 1.5
- w_out: bfloat16 [1024, 1024], P('fsdp'), may hold values from -0.1875 to 0.1875
- norm_gain2: float32 [1024], replicated, may hold values from 0.5 to 1.5
- w_gateup: bfloat16 [1024, 5632], P('fsdp'), may hold values from -0.1875 to 0.1875
- w_down: bfloat16 [2816, 1024], P('fsdp'), may hold values from -0.109375 to 0.109375
Outputs:
- output: bfloat16 [16, 1024, 1024], P(('dp', 'fsdp'), 'ctx')
- grad_inputs: bfloat16 [16, 1024, 1024], P(('dp', 'fsdp'), 'ctx')
- grad_gain1: float32 [1024], replicated
- grad_qkv: float32 [1024, 3072], P(('fsdp', 'ctx'))
- grad_beta: float32 [1024, 8], P(('fsdp', 'ctx'))
- grad_conv: float32 [4, 3072], replicated
- grad_head_gain: float32 [128], replicated
- grad_out: float32 [1024, 1024], P(('fsdp', 'ctx'))
- grad_gain2: float32 [1024], replicated
- grad_gateup: float32 [1024, 5632], P(('fsdp', 'ctx'))
- grad_down: float32 [2816, 1024], P(('fsdp', 'ctx'))
Inputs may be any that keep to these rules, and one draw needn't show every extreme that they name: `lengths`: valid tokens of each sequence; they come first in it. Some sequence has all 1024 positions valid and some sequence has 256.
All inputs are finite; a program needn't handle non-finite values.
Results may differ from a plain program's by a relative error of at most 0.014.
Values may be sent and summed in bfloat16 or wider, within the bound.
No kernel may reach another device: no remote copies, remote signals or barrier semaphores. Data moves between devices by JAX's collectives and lax.ppermute only.
A program may use at most 256 MiB of HBM per device.

v0:
```python
import jax
import jax.numpy as jnp
from jax import lax
from jax.sharding import PartitionSpec as P

H = 8
HD = 128
KERNEL = 4
SPAN = 64
exact_precision = lax.Precision.HIGHEST


def passed_along(value, axis, steps):
    count = lax.axis_size(axis)
    first, last = (max(0, -steps), min(count, count - steps))
    return lax.ppermute(value, axis, [(source, source + steps) for source in range(first, last)])


def as_sent(value):
    return jax.tree.map(lambda a: a.astype(jnp.bfloat16) if a.dtype == jnp.float32 else a, value)


def span_factors(key_row_block, value_rows, strength):
    block_len = key_row_block.shape[1]
    head_width = key_row_block.shape[2]
    gram_matrix = jnp.einsum(
        "hik,hjk->hij", key_row_block, key_row_block, precision=exact_precision
    )
    system = jnp.tril(gram_matrix * strength[:, :, None], -1) + jnp.eye(
        block_len, dtype=key_row_block.dtype
    )
    right_side = strength[:, :, None] * jnp.concatenate([key_row_block, value_rows], -1)
    solved = jax.scipy.linalg.solve_triangular(system, right_side, lower=True, unit_diagonal=True)
    return (solved[..., :head_width], solved[..., head_width:])


def span_output(memory_matrix, blocks):
    query_rows, key_row_block, value_rows, strength = blocks
    key_blend, value_blend = span_factors(key_row_block, value_rows, strength)
    prediction_error = value_blend - jnp.einsum(
        "ist,itn->isn", key_blend, memory_matrix, precision=exact_precision
    )
    scores = jnp.tril(
        jnp.einsum("hik,hjk->hij", query_rows, key_row_block, precision=exact_precision)
    )
    final_result = jnp.einsum("ist,itn->isn", query_rows, memory_matrix, precision=exact_precision)
    final_result = final_result + jnp.einsum(
        "hij,hjv->hiv", scores, prediction_error, precision=exact_precision
    )
    updated_memory = memory_matrix + jnp.einsum(
        "xzn,xzf->xnf", key_row_block, prediction_error, precision=exact_precision
    )
    return (updated_memory, final_result)


def span_advance(carry, blocks):
    memory_matrix, transition = carry
    key_row_block, value_rows, strength = blocks
    key_blend, value_blend = span_factors(key_row_block, value_rows, strength)
    prediction_error = value_blend - jnp.einsum(
        "ist,itn->isn", key_blend, memory_matrix, precision=exact_precision
    )
    memory_matrix = memory_matrix + jnp.einsum(
        "xzn,xzf->xnf", key_row_block, prediction_error, precision=exact_precision
    )
    identity = jnp.eye(key_row_block.shape[2], dtype=key_row_block.dtype)
    step_map = identity - jnp.einsum(
        "hck,hcl->hkl", key_row_block, key_blend, precision=exact_precision
    )
    transition = jnp.einsum("hij,hjk->hik", step_map, transition, precision=exact_precision)
    return ((memory_matrix, transition), None)


def to_blocks(tensor):
    shape_now = tensor.shape
    grouped = tensor.reshape((shape_now[0], shape_now[1] // SPAN, SPAN) + shape_now[2:])
    return jnp.moveaxis(grouped, 1, 0)


def from_blocks(tensor):
    moved = jnp.moveaxis(tensor, 0, 1)
    return moved.reshape((moved.shape[0], moved.shape[1] * moved.shape[2]) + moved.shape[3:])


def delta_outputs(query_rows, key_row_block, value_rows, strength, memory_matrix):
    blocks = (
        to_blocks(query_rows),
        to_blocks(key_row_block),
        to_blocks(value_rows),
        to_blocks(strength),
    )
    memory_end, outputs = lax.scan(span_output, memory_matrix, blocks)
    return (from_blocks(outputs), memory_end)


def apply_map(matrix, tensor):
    return jnp.einsum("hij,hjk->hik", matrix, tensor, precision=exact_precision)


def split_heads(tensor):
    return jnp.transpose(tensor.reshape(tensor.shape[0], H, HD), (1, 0, 2))


def join_heads(tensor):
    return jnp.transpose(tensor, (1, 0, 2)).reshape(tensor.shape[1], H * HD)


def local(
    inputs,
    lengths,
    cotangent,
    norm_gain1,
    w_qkv,
    w_beta,
    conv_weight,
    head_gain,
    w_out,
    norm_gain2,
    w_gateup,
    w_down,
):
    tokens_in = inputs[0].astype(jnp.float32)
    piece_len, model_width = tokens_in.shape
    positions = lax.axis_index("ctx") * piece_len + jnp.arange(piece_len, dtype=jnp.int32)
    valid = (positions < lengths[0]).astype(jnp.float32)
    qkv_full, beta_full, out_full = (
        lax.all_gather(w_qkv, "fsdp", axis=0, tiled=True),
        lax.all_gather(w_beta, "fsdp", axis=0, tiled=True),
        lax.all_gather(w_out, "fsdp", axis=0, tiled=True),
    )
    gateup_full, down_full = (
        lax.all_gather(w_gateup, "fsdp", axis=0, tiled=True),
        lax.all_gather(w_down, "fsdp", axis=0, tiled=True),
    )
    scale_one = lax.rsqrt(jnp.mean(tokens_in * tokens_in, -1, keepdims=True) + 1e-06)
    normed_one = (tokens_in * scale_one * norm_gain1).astype(jnp.bfloat16)
    projected = jnp.dot(normed_one, qkv_full, preferred_element_type=jnp.float32)
    beta_logits = jnp.dot(normed_one, beta_full, preferred_element_type=jnp.float32)
    conv_in = projected * valid[:, None]
    carried_rows = passed_along(
        conv_in[piece_len - KERNEL + 1 :].astype(jnp.bfloat16), "ctx", 1
    ).astype(jnp.float32)
    extended = jnp.concatenate([carried_rows, conv_in], 0)
    conv_pre = conv_weight[0] * extended[0:piece_len]
    for offset in range(1, KERNEL):
        conv_pre = conv_pre + conv_weight[offset] * extended[offset : offset + piece_len]
    gate_conv = jax.nn.sigmoid(conv_pre)
    activated = conv_pre * gate_conv
    raw_queries = split_heads(activated[:, :model_width])
    raw_keys = split_heads(activated[:, model_width : 2 * model_width])
    value_rows = split_heads(activated[:, 2 * model_width :])
    query_scale = lax.rsqrt(jnp.sum(raw_queries * raw_queries, -1, keepdims=True) + 1e-06)
    key_scale = lax.rsqrt(jnp.sum(raw_keys * raw_keys, -1, keepdims=True) + 1e-06)
    query_rows = raw_queries * query_scale * HD ** (-0.5)
    key_row_block = raw_keys * key_scale
    beta_gate = jax.nn.sigmoid(beta_logits)
    strength = jnp.transpose(beta_gate * valid[:, None])
    zero_memory = jnp.zeros((H, HD, HD), jnp.float32)
    identity = jnp.broadcast_to(jnp.eye(HD, dtype=jnp.float32), (H, HD, HD))
    advanced, _ = lax.scan(
        span_advance,
        (zero_memory, identity),
        (to_blocks(key_row_block), to_blocks(value_rows), to_blocks(strength)),
    )
    local_end, transition = advanced

    def relay_forward(step_index, memory_matrix):
        return passed_along(
            (apply_map(transition, memory_matrix) + local_end).astype(jnp.bfloat16), "ctx", 1
        ).astype(jnp.float32)

    memory_in = lax.fori_loop(0, lax.axis_size("ctx") - 1, relay_forward, zero_memory)
    (heads_out, memory_out), pull_back = jax.vjp(
        delta_outputs, query_rows, key_row_block, value_rows, strength, memory_in
    )
    head_scale = lax.rsqrt(jnp.mean(heads_out * heads_out, -1, keepdims=True) + 1e-05)
    merged = join_heads(heads_out * head_scale * head_gain).astype(jnp.bfloat16)
    attention = jnp.dot(merged, out_full, preferred_element_type=jnp.float32)
    middle = tokens_in + attention
    scale_two = lax.rsqrt(jnp.mean(middle * middle, -1, keepdims=True) + 1e-06)
    normed_two = (middle * scale_two * norm_gain2).astype(jnp.bfloat16)
    gate_up = jnp.dot(normed_two, gateup_full, preferred_element_type=jnp.float32)
    ff_width = gate_up.shape[1] // 2
    gate_part = gate_up[:, :ff_width]
    up_part = gate_up[:, ff_width:]
    gate_sig = jax.nn.sigmoid(gate_part)
    hidden = (gate_part * gate_sig * up_part).astype(jnp.bfloat16)
    feed_out = jnp.dot(hidden, down_full, preferred_element_type=jnp.float32)
    output = (middle + feed_out).astype(jnp.bfloat16)
    qkv_back, beta_back, out_back = (
        lax.all_gather(w_qkv, "fsdp", axis=0, tiled=True),
        lax.all_gather(w_beta, "fsdp", axis=0, tiled=True),
        lax.all_gather(w_out, "fsdp", axis=0, tiled=True),
    )
    gateup_back, down_back = (
        lax.all_gather(w_gateup, "fsdp", axis=0, tiled=True),
        lax.all_gather(w_down, "fsdp", axis=0, tiled=True),
    )
    contract_cols = (((1,), (1,)), ((), ()))
    masked_cotangent = cotangent[0].astype(jnp.float32) * valid[:, None]
    grad_feed = masked_cotangent.astype(jnp.bfloat16)
    grad_hidden = lax.dot_general(
        grad_feed, down_back, contract_cols, preferred_element_type=jnp.float32
    )
    grad_gate = grad_hidden * up_part * gate_sig * (1.0 + gate_part * (1.0 - gate_sig))
    grad_up = grad_hidden * gate_part * gate_sig
    grad_gate_up = jnp.concatenate([grad_gate, grad_up], 1).astype(jnp.bfloat16)
    grad_normed_two = lax.dot_general(
        grad_gate_up, gateup_back, contract_cols, preferred_element_type=jnp.float32
    )
    gain_two_term = jnp.sum(grad_normed_two * middle * scale_two, 0)
    scaled_two = grad_normed_two * norm_gain2
    grad_middle = (
        masked_cotangent
        + scale_two * scaled_two
        - scale_two
        * scale_two
        * scale_two
        * middle
        * jnp.mean(scaled_two * middle, -1, keepdims=True)
    )
    grad_attention = grad_middle.astype(jnp.bfloat16)
    grad_merged = lax.dot_general(
        grad_attention, out_back, contract_cols, preferred_element_type=jnp.float32
    )
    grad_heads = split_heads(grad_merged)
    head_gain_term = jnp.sum(grad_heads * heads_out * head_scale, (0, 1))
    scaled_heads = grad_heads * head_gain
    grad_heads_out = (
        head_scale * scaled_heads
        - head_scale
        * head_scale
        * head_scale
        * heads_out
        * jnp.mean(scaled_heads * heads_out, -1, keepdims=True)
    )
    local_grads = pull_back((grad_heads_out, jnp.zeros_like(memory_out)))
    local_part = local_grads[4]
    transposed = jnp.transpose(transition, (0, 2, 1))

    def relay_backward(step_index, memory_grad):
        return passed_along(
            (apply_map(transposed, memory_grad) + local_part).astype(jnp.bfloat16), "ctx", -1
        ).astype(jnp.float32)

    grad_memory_out = lax.fori_loop(0, lax.axis_size("ctx") - 1, relay_backward, zero_memory)
    grad_queries, grad_keys, grad_values, grad_strength, _ = pull_back(
        (grad_heads_out, grad_memory_out)
    )
    grad_beta_logits = (
        jnp.transpose(grad_strength) * valid[:, None] * beta_gate * (1.0 - beta_gate)
    ).astype(jnp.bfloat16)
    grad_raw_queries = HD ** (-0.5) * (
        query_scale * grad_queries
        - query_scale
        * query_scale
        * query_scale
        * raw_queries
        * jnp.sum(raw_queries * grad_queries, -1, keepdims=True)
    )
    grad_raw_keys = key_scale * grad_keys - key_scale * key_scale * key_scale * raw_keys * jnp.sum(
        raw_keys * grad_keys, -1, keepdims=True
    )
    grad_activated = jnp.concatenate(
        [join_heads(grad_raw_queries), join_heads(grad_raw_keys), join_heads(grad_values)], 1
    )
    grad_conv_pre = grad_activated * gate_conv * (1.0 + conv_pre * (1.0 - gate_conv))
    conv_rows = [
        jnp.sum(grad_conv_pre * extended[offset : offset + piece_len], 0)
        for offset in range(KERNEL)
    ]
    conv_term = jnp.stack(conv_rows, 0)
    grad_extended = jnp.pad(conv_weight[0] * grad_conv_pre, ((0, KERNEL - 1), (0, 0)))
    for offset in range(1, KERNEL):
        grad_extended = grad_extended + jnp.pad(
            conv_weight[offset] * grad_conv_pre, ((offset, KERNEL - 1 - offset), (0, 0))
        )
    returned_rows = passed_along(as_sent(grad_extended[: KERNEL - 1]), "ctx", -1)
    grad_conv_in = grad_extended[KERNEL - 1 :] + jnp.pad(
        returned_rows, ((piece_len - KERNEL + 1, 0), (0, 0))
    )
    grad_projected = (grad_conv_in * valid[:, None]).astype(jnp.bfloat16)
    grad_normed_one = lax.dot_general(
        grad_projected, qkv_back, contract_cols, preferred_element_type=jnp.float32
    )
    grad_normed_one = grad_normed_one + lax.dot_general(
        grad_beta_logits, beta_back, contract_cols, preferred_element_type=jnp.float32
    )
    gain_one_term = jnp.sum(grad_normed_one * tokens_in * scale_one, 0)
    scaled_one = grad_normed_one * norm_gain1
    grad_tokens = (
        grad_middle
        + scale_one * scaled_one
        - scale_one
        * scale_one
        * scale_one
        * tokens_in
        * jnp.mean(scaled_one * tokens_in, -1, keepdims=True)
    )
    contract_rows = (((0,), (0,)), ((), ()))
    parts = [
        lax.dot_general(
            normed_one, grad_projected, contract_rows, preferred_element_type=jnp.float32
        ),
        lax.dot_general(merged, grad_attention, contract_rows, preferred_element_type=jnp.float32),
        lax.dot_general(
            normed_two, grad_gate_up, contract_rows, preferred_element_type=jnp.float32
        ),
        lax.dot_general(
            normed_one, grad_beta_logits, contract_rows, preferred_element_type=jnp.float32
        ),
    ]
    wide_share = lax.psum_scatter(
        jnp.concatenate(parts, 1), ("fsdp", "ctx"), scatter_dimension=0, tiled=True
    )
    down_share = lax.psum_scatter(
        lax.dot_general(hidden, grad_feed, contract_rows, preferred_element_type=jnp.float32),
        ("fsdp", "ctx"),
        scatter_dimension=0,
        tiled=True,
    )
    small_sums = lax.psum(
        (gain_one_term, conv_term, head_gain_term, gain_two_term), ("fsdp", "ctx")
    )
    totals = (
        lax.psum(wide_share.astype(jnp.bfloat16), "dp").astype(jnp.float32),
        lax.psum(down_share.astype(jnp.bfloat16), "dp").astype(jnp.float32),
        lax.psum(small_sums[0].astype(jnp.bfloat16), "dp").astype(jnp.float32),
        lax.psum(small_sums[1].astype(jnp.bfloat16), "dp").astype(jnp.float32),
        lax.psum(small_sums[2].astype(jnp.bfloat16), "dp").astype(jnp.float32),
        lax.psum(small_sums[3].astype(jnp.bfloat16), "dp").astype(jnp.float32),
    )
    wide_total = totals[0]
    qkv_cols = 3 * model_width
    out_end = qkv_cols + model_width
    gateup_end = out_end + gate_up.shape[1]
    return (
        output[None],
        grad_tokens.astype(jnp.bfloat16)[None],
        totals[2],
        wide_total[:, :qkv_cols],
        wide_total[:, gateup_end:],
        totals[3],
        totals[4],
        wide_total[:, qkv_cols:out_end],
        totals[5],
        wide_total[:, out_end:gateup_end],
        totals[1],
    )


def solution(mesh):
    placed = (
        P(("dp", "fsdp"), "ctx", None),
        P(("dp", "fsdp")),
        P(("dp", "fsdp"), "ctx", None),
        P(),
        P("fsdp", None),
        P("fsdp", None),
        P(),
        P(),
        P("fsdp", None),
        P(),
        P("fsdp", None),
        P("fsdp", None),
    )
    return jax.shard_map(
        local,
        mesh=mesh,
        in_specs=placed,
        out_specs=(
            P(("dp", "fsdp"), "ctx", None),
            P(("dp", "fsdp"), "ctx", None),
            P(),
            P(("fsdp", "ctx"), None),
            P(("fsdp", "ctx"), None),
            P(),
            P(),
            P(("fsdp", "ctx"), None),
            P(),
            P(("fsdp", "ctx"), None),
            P(("fsdp", "ctx"), None),
        ),
        check_vma=False,
    )
```

profile of v0, /device:TPU:0, one launch (start us, length us, event | category | flops | bytes accessed | tf_op | source)
XLA Modules:
  0.0 2306.2 jit_solution(14385309891945264913)
XLA Ops:
  11.7 14.9 all_gather.21
  27.2 100.5 %all-gather.5.cloned.1.call-done = bf16[1024,3072]{1,0:T(8,128)(2,1)} async-done(((bf16[256,3072]{1,0:T(8,128)(2,1)}), bf16[1024,3072]{1,0:T(8,128)(2,1)}) %all-gather.5.cloned.1.call-update) | async-done | bytes 6291472 | tf_op jit(solution)/shard_map/all_gather | solution.py:127
  127.7 5.6 convolution_multiply_fusion.1
  133.4 2.6 copy-done.13
  138.9 12.9 fusion.151
  159.1 413.5 %while.99 = (s32[]{:T(128)}, f32[8,128,128]{2,1,0:T(8,128)S(1)}, f32[8,128,128]{2,1,0:T(8,128)}, f32[8,8,64,128]{3,2,1,0:T(8,128)S(1)}, f32[8,8,64]{2,1,0:T(8,12...) while((s32[]{:T(128)}, f32[8,128,128]{2,1,0:T(8,128)S(1)}, ...), condition=%wide.region_3.5_spmd.clone, body=%wide.region_2.4_spmd.clone.sunk | while | flops 655380544 | bytes 13583016 | solution.py:160
  162.2 40.7 %custom-call.39 = f32[8,1,64,64]{2,3,1,0:T(8,128)} custom-call(f32[8,1,64,64]{3,2,1,0:T(8,128)} %fusion.417), custom_call_target="InvertDiagBlocksLowerTriangular" | custom-call | tf_op jit(solution)/shard_map/while/body/eval_jaxpr/jit(_solve_triangular)/vmap()/triangular_solve/custom-call.1 | solution.py:33
  213.9 40.7 %custom-call.39 = f32[8,1,64,64]{2,3,1,0:T(8,128)} custom-call(f32[8,1,64,64]{3,2,1,0:T(8,128)} %fusion.417), custom_call_target="InvertDiagBlocksLowerTriangular" | custom-call | tf_op jit(solution)/shard_map/while/body/eval_jaxpr/jit(_solve_triangular)/vmap()/triangular_solve/custom-call.1 | solution.py:33
  265.6 40.7 %custom-call.39 = f32[8,1,64,64]{2,3,1,0:T(8,128)} custom-call(f32[8,1,64,64]{3,2,1,0:T(8,128)} %fusion.417), custom_call_target="InvertDiagBlocksLowerTriangular" | custom-call | tf_op jit(solution)/shard_map/while/body/eval_jaxpr/jit(_solve_triangular)/vmap()/triangular_solve/custom-call.1 | solution.py:33
  317.2 40.7 %custom-call.39 = f32[8,1,64,64]{2,3,1,0:T(8,128)} custom-call(f32[8,1,64,64]{3,2,1,0:T(8,128)} %fusion.417), custom_call_target="InvertDiagBlocksLowerTriangular" | custom-call | tf_op jit(solution)/shard_map/while/body/eval_jaxpr/jit(_solve_triangular)/vmap()/triangular_solve/custom-call.1 | solution.py:33
  368.9 40.7 %custom-call.39 = f32[8,1,64,64]{2,3,1,0:T(8,128)} custom-call(f32[8,1,64,64]{3,2,1,0:T(8,128)} %fusion.417), custom_call_target="InvertDiagBlocksLowerTriangular" | custom-call | tf_op jit(solution)/shard_map/while/body/eval_jaxpr/jit(_solve_triangular)/vmap()/triangular_solve/custom-call.1 | solution.py:33
  420.6 40.7 %custom-call.39 = f32[8,1,64,64]{2,3,1,0:T(8,128)} custom-call(f32[8,1,64,64]{3,2,1,0:T(8,128)} %fusion.417), custom_call_target="InvertDiagBlocksLowerTriangular" | custom-call | tf_op jit(solution)/shard_map/while/body/eval_jaxpr/jit(_solve_triangular)/vmap()/triangular_solve/custom-call.1 | solution.py:33
  472.3 40.7 %custom-call.39 = f32[8,1,64,64]{2,3,1,0:T(8,128)} custom-call(f32[8,1,64,64]{3,2,1,0:T(8,128)} %fusion.417), custom_call_target="InvertDiagBlocksLowerTriangular" | custom-call | tf_op jit(solution)/shard_map/while/body/eval_jaxpr/jit(_solve_triangular)/vmap()/triangular_solve/custom-call.1 | solution.py:33
  524.0 40.7 %custom-call.39 = f32[8,1,64,64]{2,3,1,0:T(8,128)} custom-call(f32[8,1,64,64]{3,2,1,0:T(8,128)} %fusion.417), custom_call_target="InvertDiagBlocksLowerTriangular" | custom-call | tf_op jit(solution)/shard_map/while/body/eval_jaxpr/jit(_solve_triangular)/vmap()/triangular_solve/custom-call.1 | solution.py:33
  583.0 469.8 %while.97 = (s32[]{:T(128)}, f32[8,128,128]{2,1,0:T(8,128)S(1)}, f32[8,8,64,128]{3,2,0,1:T(8,128)}, f32[8,8,64,1]{2,1,3,0:T(8,128)S(1)}, f32[8,8,64,64]{3,2,1,0:...) while((s32[]{:T(128)}, f32[8,128,128]{2,1,0:T(8,128)S(1)}, ...), condition=%wide.region_6.8_spmd.clone, body=%wide.region_5.7_spmd.clone.sunk | while | flops 554618944 | bytes 16134973 | solution.py:92
  590.1 40.7 %custom-call.37 = f32[8,1,64,64]{2,3,1,0:T(8,128)} custom-call(f32[8,1,64,64]{3,2,1,0:T(8,128)} %add_bitcast_fusion.4), custom_call_target="InvertDiagBlocksLowerTriangular" | custom-call | tf_op jit(solution)/shard_map/jvp()/while/body/eval_jaxpr/jit(_solve_triangular)/vmap()/triangular_solve/custom-call.1 | solution.py:33
  648.7 40.7 %custom-call.37 = f32[8,1,64,64]{2,3,1,0:T(8,128)} custom-call(f32[8,1,64,64]{3,2,1,0:T(8,128)} %add_bitcast_fusion.4), custom_call_target="InvertDiagBlocksLowerTriangular" | custom-call | tf_op jit(solution)/shard_map/jvp()/while/body/eval_jaxpr/jit(_solve_triangular)/vmap()/triangular_solve/custom-call.1 | solution.py:33
  707.5 40.7 %custom-call.37 = f32[8,1,64,64]{2,3,1,0:T(8,128)} custom-call(f32[8,1,64,64]{3,2,1,0:T(8,128)} %add_bitcast_fusion.4), custom_call_target="InvertDiagBlocksLowerTriangular" | custom-call | tf_op jit(solution)/shard_map/jvp()/while/body/eval_jaxpr/jit(_solve_triangular)/vmap()/triangular_solve/custom-call.1 | solution.py:33
  766.3 40.7 %custom-call.37 = f32[8,1,64,64]{2,3,1,0:T(8,128)} custom-call(f32[8,1,64,64]{3,2,1,0:T(8,128)} %add_bitcast_fusion.4), custom_call_target="InvertDiagBlocksLowerTriangular" | custom-call | tf_op jit(solution)/shard_map/jvp()/while/body/eval_jaxpr/jit(_solve_triangular)/vmap()/triangular_solve/custom-call.1 | solution.py:33
  807.0 2.6 bitcast_dynamic-update-slice_fusion.16
  825.0 40.7 %custom-call.37 = f32[8,1,64,64]{2,3,1,0:T(8,128)} custom-call(f32[8,1,64,64]{3,2,1,0:T(8,128)} %add_bitcast_fusion.4), custom_call_target="InvertDiagBlocksLowerTriangular" | custom-call | tf_op jit(solution)/shard_map/jvp()/while/body/eval_jaxpr/jit(_solve_triangular)/vmap()/triangular_solve/custom-call.1 | solution.py:33
  883.8 40.7 %custom-call.37 = f32[8,1,64,64]{2,3,1,0:T(8,128)} custom-call(f32[8,1,64,64]{3,2,1,0:T(8,128)} %add_bitcast_fusion.4), custom_call_target="InvertDiagBlocksLowerTriangular" | custom-call | tf_op jit(solution)/shard_map/jvp()/while/body/eval_jaxpr/jit(_solve_triangular)/vmap()/triangular_solve/custom-call.1 | solution.py:33
  942.5 40.7 %custom-call.37 = f32[8,1,64,64]{2,3,1,0:T(8,128)} custom-call(f32[8,1,64,64]{3,2,1,0:T(8,128)} %add_bitcast_fusion.4), custom_call_target="InvertDiagBlocksLowerTriangular" | custom-call | tf_op jit(solution)/shard_map/jvp()/while/body/eval_jaxpr/jit(_solve_triangular)/vmap()/triangular_solve/custom-call.1 | solution.py:33
  1001.2 40.7 %custom-call.37 = f32[8,1,64,64]{2,3,1,0:T(8,128)} custom-call(f32[8,1,64,64]{3,2,1,0:T(8,128)} %add_bitcast_fusion.4), custom_call_target="InvertDiagBlocksLowerTriangular" | custom-call | tf_op jit(solution)/shard_map/jvp()/while/body/eval_jaxpr/jit(_solve_triangular)/vmap()/triangular_solve/custom-call.1 | solution.py:33
  1055.2 2.7 fusion.189
  1060.1 4.8 multiply_reduce_fusion.6
  1065.0 12.3 fusion.218
  1077.3 11.9 multiply_convert_fusion.1
  1091.8 11.1 fusion.152
  1102.9 13.4 multiply_reduce_fusion.4
  1126.1 48.7 %while.100 = (s32[]{:T(128)}, f32[8,128,128]{2,1,0:T(8,128)S(1)}, f32[8,8,64,128]{3,2,1,0:T(8,128)}, f32[8,8,64,128]{3,2,1,0:T(8,128)}, f32[8,8,64,128]{3,2,1,0:...) while((s32[]{:T(128)}, f32[8,128,128]{2,1,0:T(8,128)S(1)}, ...), condition=%wide.region_12.14_spmd.clone, body=%wide.region_11.13_spmd.clone.sunk | while | flops 352976896 | bytes 5245579 | solution.py:92
  1177.1 9.6 fusion.204
  1187.9 4.9 fusion.201
  1198.8 541.7 %while.98 = (s32[]{:T(128)}, f32[8,128,128]{2,1,0:T(8,128)S(1)}, f32[8,8,64,128]{3,2,0,1:T(8,128)}, f32[8,8,64,128]{3,2,0,1:T(8,128)}, f32[8,8,64,128]{3,2,0,1:T...) while((s32[]{:T(128)}, f32[8,128,128]{2,1,0:T(8,128)S(1)}, ...), condition=%wide.region_16.18_spmd.clone.clone, body=%wide.region_13.17_spmd.clone.clone.sunk | while | flops 1134243328 | bytes 18174760 | solution.py:92
  1199.0 2.8 fusion.396
  1216.7 40.7 %custom-call.38 = f32[8,1,64,64]{2,3,1,0:T(8,128)} custom-call(f32[8,1,64,64]{3,2,1,0:T(8,128)} %add_bitcast_fusion.5), custom_call_target="InvertDiagBlocksLowerTriangular" | custom-call | tf_op jit(solution)/shard_map/transpose(jvp())/while/body/eval_jaxpr/jit(_solve_triangular)/vmap()/triangular_solve | solution.py:33
  1266.8 2.8 fusion.396
  1284.5 40.7 %custom-call.38 = f32[8,1,64,64]{2,3,1,0:T(8,128)} custom-call(f32[8,1,64,64]{3,2,1,0:T(8,128)} %add_bitcast_fusion.5), custom_call_target="InvertDiagBlocksLowerTriangular" | custom-call | tf_op jit(solution)/shard_map/transpose(jvp())/while/body/eval_jaxpr/jit(_solve_triangular)/vmap()/triangular_solve | solution.py:33
  1334.5 2.8 fusion.396
  1352.1 40.7 %custom-call.38 = f32[8,1,64,64]{2,3,1,0:T(8,128)} custom-call(f32[8,1,64,64]{3,2,1,0:T(8,128)} %add_bitcast_fusion.5), custom_call_target="InvertDiagBlocksLowerTriangular" | custom-call | tf_op jit(solution)/shard_map/transpose(jvp())/while/body/eval_jaxpr/jit(_solve_triangular)/vmap()/triangular_solve | solution.py:33
  1402.2 2.8 fusion.396
  1419.8 40.7 %custom-call.38 = f32[8,1,64,64]{2,3,1,0:T(8,128)} custom-call(f32[8,1,64,64]{3,2,1,0:T(8,128)} %add_bitcast_fusion.5), custom_call_target="InvertDiagBlocksLowerTriangular" | custom-call | tf_op jit(solution)/shard_map/transpose(jvp())/while/body/eval_jaxpr/jit(_solve_triangular)/vmap()/triangular_solve | solution.py:33
  1469.8 2.8 fusion.396
  1487.5 40.7 %custom-call.38 = f32[8,1,64,64]{2,3,1,0:T(8,128)} custom-call(f32[8,1,64,64]{3,2,1,0:T(8,128)} %add_bitcast_fusion.5), custom_call_target="InvertDiagBlocksLowerTriangular" | custom-call | tf_op jit(solution)/shard_map/transpose(jvp())/while/body/eval_jaxpr/jit(_solve_triangular)/vmap()/triangular_solve | solution.py:33
  1537.5 2.8 fusion.396
  1555.2 40.7 %custom-call.38 = f32[8,1,64,64]{2,3,1,0:T(8,128)} custom-call(f32[8,1,64,64]{3,2,1,0:T(8,128)} %add_bitcast_fusion.5), custom_call_target="InvertDiagBlocksLowerTriangular" | custom-call | tf_op jit(solution)/shard_map/transpose(jvp())/while/body/eval_jaxpr/jit(_solve_triangular)/vmap()/triangular_solve | solution.py:33
  1605.2 2.8 fusion.396
  1622.9 40.7 %custom-call.38 = f32[8,1,64,64]{2,3,1,0:T(8,128)} custom-call(f32[8,1,64,64]{3,2,1,0:T(8,128)} %add_bitcast_fusion.5), custom_call_target="InvertDiagBlocksLowerTriangular" | custom-call | tf_op jit(solution)/shard_map/transpose(jvp())/while/body/eval_jaxpr/jit(_solve_triangular)/vmap()/triangular_solve | solution.py:33
  1672.9 2.8 fusion.396
  1690.6 40.7 %custom-call.38 = f32[8,1,64,64]{2,3,1,0:T(8,128)} custom-call(f32[8,1,64,64]{3,2,1,0:T(8,128)} %add_bitcast_fusion.5), custom_call_target="InvertDiagBlocksLowerTriangular" | custom-call | tf_op jit(solution)/shard_map/transpose(jvp())/while/body/eval_jaxpr/jit(_solve_triangular)/vmap()/triangular_solve | solution.py:33
  1743.5 2.8 fusion.167
  1753.5 5.7 multiply_reduce_fusion.3
  1759.3 6.9 broadcast_multiply_fusion.4
  1766.2 8.1 pad_add_fusion.3
  1778.0 6.9 fusion.221
  1784.9 26.0 %pad_maximum_fusion.2 = f32[1024,9736]{1,0:T(8,128)} fusion(f32[1024,8]{1,0:T(8,128)S(1)} %fusion.219, f32[1024,5632]{1,0:T(8,128)} %fusion.152, f32[1024,1024]{1,0:T(8,128)S(1)} %copy-done.10, f32[1024,3072]{1,0:T(8,128)} %fusion.221), kind=kLoop, calls=%fused_computation.201 | loop fusion | flops 29908992 | bytes 79757312 | tf_op jit(solution)/shard_map/concatenate | solution.py:314
  1813.7 385.5 %reduce-scatter.3.cloned.1.call-done = f32[128,9736]{1,0:T(8,128)} async-done(((f32[1024,9736]{1,0:T(8,128)}), f32[128,9736]{1,0:T(8,128)}) %reduce-scatter.3.cloned.1.call-update) | async-done | bytes 4984848 | tf_op jit(solution)/shard_map/reduce_scatter | solution.py:313
  2199.2 4.1 convert_element_type.180
  2204.9 8.7 fusion.194
  2214.2 10.1 fusion.162
  2224.3 26.4 %all-reduce.7 = (bf16[1024]{0:T(1024)(128)(2,1)S(1)}, bf16[4,3072]{1,0:T(4,128)(2,1)S(1)}, bf16[128]{0:T(256)(128)(2,1)S(1)}, bf16[1024]{0:T(1024)(128)(2,1)S(1)}) all-reduce(f32[1024]{0:T(1024)S(1)} %get-tuple-element.1318, f32[4,3072]{1,0:T(4,128)S(1)} %pad_maximum_fusion.7, ...), channel_id=1, replica_groups=mesh['dp'=4,'fsdp'=4,'ctx'=2] {'fsdp','ctx'}, use_global_device_ids=true, to_apply=%region_21.23 | all-reduce | flops 14464 | bytes 86784 | tf_op jit(solution)/shard_map/psum | solution.py:322
  2250.7 16.6 all-reduce.8
  2269.6 3.4 fusion.200
  2273.0 18.6 all-reduce.12.cloned.1.call-done
  (763 shorter events, 548.8 us)
Async XLA Ops:
  7.2 120.5 %all-gather.5.cloned.1.call-start = ((), (), s32[]{:S(2)}) async-start(), calls=%async_computation.2 | async-start | bytes 7864320 | tf_op jit(solution)/shard_map/all_gather | solution.py:127
  7.9 1052.2 %all-gather.7.cloned.1.call-start = ((), (), s32[]{:S(2)}) async-start(), calls=%async_computation.3 | async-start | bytes 2621440 | tf_op jit(solution)/shard_map/all_gather | solution.py:129
  8.7 18.0 copy-start.55
  8.7 1056.3 %all-gather.9.cloned.1.call-start = ((), (), s32[]{:S(2)}) async-start(), calls=%async_computation.4 | async-start | bytes 14417920 | tf_op jit(solution)/shard_map/all_gather | solution.py:132
  9.4 1067.9 %all-gather.11.cloned.1.call-start = ((), (), s32[]{:S(2)}) async-start(), calls=%async_computation.5 | async-start | bytes 7208960 | tf_op jit(solution)/shard_map/all_gather | solution.py:133
  10.0 1801.3 %reduce-scatter.5.cloned.1.call-start = ((), (), s32[]{:S(2)}) async-start(), calls=%async_computation.7 | async-start | bytes 12976128 | tf_op jit(solution)/shard_map/reduce_scatter | solution.py:316
  11.6 121.7 %copy-start.50 = (f32[512]{0:T(512)}, f32[512]{0:T(512)S(1)}, u32[]{:S(2)}) copy-start(f32[512]{0:T(512)S(1)} %get-tuple-element.1475) | copy-start | bytes 6148
  11.7 127.2 %copy-start.35 = (f32[1,3072]{1,0:T(1,128)}, f32[1,3072]{1,0:T(1,128)S(1)}, u32[]{:S(2)}) copy-start(f32[1,3072]{1,0:T(1,128)S(1)} %get-tuple-element.1466) | copy-start | bytes 36868
  11.7 127.2 %copy-start.37 = (f32[1,3072]{1,0:T(1,128)}, f32[1,3072]{1,0:T(1,128)S(1)}, u32[]{:S(2)}) copy-start(f32[1,3072]{1,0:T(1,128)S(1)} %get-tuple-element.1467) | copy-start | bytes 36868
  11.7 127.2 %copy-start.39 = (f32[1,3072]{1,0:T(1,128)}, f32[1,3072]{1,0:T(1,128)S(1)}, u32[]{:S(2)}) copy-start(f32[1,3072]{1,0:T(1,128)S(1)} %get-tuple-element.1468) | copy-start | bytes 36868
  11.7 127.2 %copy-start.41 = (f32[1,3072]{1,0:T(1,128)}, f32[1,3072]{1,0:T(1,128)S(1)}, u32[]{:S(2)}) copy-start(f32[1,3072]{1,0:T(1,128)S(1)} %get-tuple-element.1469) | copy-start | bytes 36868
  26.6 106.8 %copy-start.44 = (bf16[1024,8]{0,1:T(8,128)(2,1)}, bf16[1024,8]{0,1:T(8,128)(2,1)S(1)}, u32[]{:S(2)}) copy-start(bf16[1024,8]{0,1:T(8,128)(2,1)S(1)} %all_gather.21) | copy-start | bytes 49156
  27.2 106.2 %copy-start.46 = (f32[512,8]{0,1:T(8,128)}, f32[512,8]{0,1:T(8,128)S(1)}, u32[]{:S(2)}) copy-start(f32[512,8]{0,1:T(8,128)S(1)} %fusion.199) | copy-start | bytes 49156
  136.0 2.8 collective-permute-start
  138.8 13.0 copy-start.30
  205.4 3.8 copy-start.8
  308.8 3.8 copy-start.8
  412.2 3.8 copy-start.8
  572.6 6.5 copy-start.4
  574.4 6.9 collective-permute-start.1
  633.3 4.9 copy-start.1
  692.0 3.9 copy-start.11
  692.0 5.0 copy-start.1
  750.8 3.9 copy-start.11
  750.8 5.0 copy-start.1
  809.6 3.8 copy-start.11
  809.6 5.0 copy-start.1
  868.3 3.8 copy-start.11
  868.3 5.0 copy-start.1
  927.1 3.9 copy-start.11
  927.1 5.0 copy-start.1
  985.8 3.8 copy-start.11
  985.8 4.9 copy-start.1
  1044.5 5.0 copy-start.1
  1060.1 4.8 copy-start.32
  1077.3 14.5 copy-start.16
  1102.9 13.4 copy-start.28
  1126.1 48.7 %copy-start.9 = (f32[8,128,128]{2,1,0:T(8,128)S(1)}, f32[8,128,128]{2,1,0:T(8,128)}, u32[]{:S(2)}) copy-start(f32[8,128,128]{2,1,0:T(8,128)} %get-tuple-element.962) | copy-start | bytes 1572868
  1175.8 17.1 collective-permute-start.2
  1186.8 1012.4 %reduce-scatter.3.cloned.1.call-start = ((), (), s32[]{:S(2)}) async-start(), calls=%async_computation.6 | async-start | bytes 45416448 | tf_op jit(solution)/shard_map/reduce_scatter | solution.py:313
  1257.4 5.2 copy-start.12
  1325.2 5.2 copy-start.12
  1392.8 5.2 copy-start.12
  1460.5 5.2 copy-start.12
  1528.2 5.2 copy-start.12
  1595.9 5.2 copy-start.12
  1663.6 5.2 copy-start.12
  1731.3 5.2 copy-start.12
  1746.3 6.1 slice-start.2
  1753.5 5.8 copy-start.36
  1753.5 5.8 copy-start.38
  1753.5 5.8 copy-start.40
  1753.5 5.8 copy-start.42
  1766.2 9.4 copy-start.47
  1766.2 9.5 copy-start.23
  1766.2 9.5 copy-start.51
  1766.2 9.5 copy-start.56
  1774.4 3.7 collective-permute-start.3
  1778.0 6.9 copy-start.10
  1811.0 480.7 %all-reduce.12.cloned.1.call-start = ((), (), s32[]{:S(2)}) async-start(), calls=%async_computation.8 | async-start | bytes 6488064 | tf_op jit(solution)/shard_map/psum | solution.py:326
  2204.9 8.7 copy-start.45
  2214.2 10.1 copy-start.53
  2214.2 55.5 %copy-start.15 = (f32[512,1024]{1,0:T(8,128)S(1)}, f32[512,1024]{1,0:T(8,128)}, u32[]{:S(2)}) copy-start(f32[512,1024]{1,0:T(8,128)} %copy-done.14) | copy-start | bytes 6291460
  2214.2 55.5 %copy-start.49 = (f32[512]{0:T(512)S(1)}, f32[512]{0:T(512)}, u32[]{:S(2)}) copy-start(f32[512]{0:T(512)} %get-tuple-element.1474) | copy-start | bytes 6148
  (50 other events, 126.1 us)
Sparse Core Ops, SparseCore 0:
  9.6 118.0 all-gather.4
  129.3 44.1 all-gather.6
  175.0 200.9 all-gather.8
  377.4 104.9 all-gather.10
  1186.9 118.9 reduce-scatter.4
  1811.1 388.0 reduce-scatter.2
  2203.5 88.1 all-reduce.11
where the time goes:
time: 2320 us; the launch traced here: 2310 us
  other arithmetic  1100 us (47%)
  matrix products  510 us (22%)
  waiting for transfers between devices  509 us (22%)
  local copies, waits for them, and re-layouts  97.5 us (4%)
  blocking collectives  57.9 us (2%)
    another operation x96, other arithmetic, span_factors(): jax.scipy.linalg.solve_triangular(system, right_side, lower=True, unit_di...  999 us
    reduce_scatter x1, waiting for transfers between devices, local(): lax.psum_scatter(jnp.concatenate(parts, 1), ('fsdp', 'ctx'), scatter_dime...  386 us
    all_gather x1, waiting for transfers between devices, local(): lax.all_gather(w_qkv, 'fsdp', axis=0, tiled=True)  101 us
    another operation x32, matrix products, span_factors(): jax.scipy.linalg.solve_triangular(system, right_side, lower=True, unit_di...  68.7 us
    dot_general x32, matrix products, span_output(): jnp.einsum('ist,itn->isn', query_rows, memory_matrix, precision=exact_pre...  68.5 us
    dot_general x32, matrix products, span_output(): jnp.einsum('ist,itn->isn', key_blend, memory_matrix, precision=exact_prec...  59 us
  transfers between devices with their start and end apart: 11, of which 5 were waited for; matrix products, arithmetic and copies ran while one was open for 69% of the time, Pallas kernels for 0%

commit v1 on v0

--- a/solution.py
+++ b/solution.py
@@ -8,6 +8,22 @@
 KERNEL = 4
 SPAN = 64
 exact_precision = lax.Precision.HIGHEST
+
+
+def gather_around(x, axis, dim):
+    ways, here, turn = (lax.axis_size(axis), lax.axis_index(axis), x.shape[dim])
+    dims = [n * ways if d == dim else n for d, n in enumerate(x.shape)]
+    full = lax.dynamic_update_slice_in_dim(jnp.zeros(dims, x.dtype), x, here * turn, axis=dim)
+    going_up = going_down = x
+    for far in range(1, ways // 2 + 1):
+        going_up = lax.ppermute(going_up, axis, [(d, (d + 1) % ways) for d in range(ways)])
+        full = lax.dynamic_update_slice_in_dim(full, going_up, (here - far) % ways * turn, axis=dim)
+        if 2 * far < ways:
+            going_down = lax.ppermute(going_down, axis, [(d, (d - 1) % ways) for d in range(ways)])
+            full = lax.dynamic_update_slice_in_dim(
+                full, going_down, (here + far) % ways * turn, axis=dim
+            )
+    return full
 
 
 def passed_along(value, axis, steps):
@@ -124,7 +140,7 @@
     positions = lax.axis_index("ctx") * piece_len + jnp.arange(piece_len, dtype=jnp.int32)
     valid = (positions < lengths[0]).astype(jnp.float32)
     qkv_full, beta_full, out_full = (
-        lax.all_gather(w_qkv, "fsdp", axis=0, tiled=True),
+        gather_around(w_qkv, "fsdp", 0),
         lax.all_gather(w_beta, "fsdp", axis=0, tiled=True),
         lax.all_gather(w_out, "fsdp", axis=0, tiled=True),
     )

time: 2320 us -> 2550 us (1.099)
  waiting for transfers between devices: 509 us -> 623 us
  blocking collectives: 57.9 us -> 160 us
    all_gather x1, blocking collectives: 14.9 us -> 117 us  [local(): lax.all_gather(w_beta, 'fsdp', axis=0, tiled=True)]
    ppermute x0 -> x3, waiting for transfers between devices: none -> 65.4 us  [the longest x2 65.4 us: gather_around(): lax.ppermute(going_up, axis, [(d, (d + 1) % ways) for d in range(ways)])]
    reduce_scatter x1, waiting for transfers between devices: 386 us -> 421 us  [local(): lax.psum_scatter(jnp.concatenate(parts, 1), ('fsdp', 'ctx'), scatter_dime...]
  transfers between devices with their start and end apart: 11 -> 14, of which waited for: 5 -> 6; matrix products, arithmetic and copies ran while one was open for 69% -> 63% of each run, Pallas kernels for 0% -> 0%
where the time goes in v1:
time: 2550 us; the launch traced here: 2540 us
  other arithmetic  1100 us (43%)
  waiting for transfers between devices  623 us (24%)
  matrix products  511 us (20%)
  blocking collectives  160 us (6%)
  local copies, waits for them, and re-layouts  110 us (4%)
    another operation x96, other arithmetic, span_factors(): jax.scipy.linalg.solve_triangular(system, right_side, lower=True, unit_di...  999 us
    reduce_scatter x1, waiting for transfers between devices, local(): lax.psum_scatter(jnp.concatenate(parts, 1), ('fsdp', 'ctx'), scatter_dime...  421 us
    all_gather x1, blocking collectives, local(): lax.all_gather(w_beta, 'fsdp', axis=0, tiled=True)  117 us
    all_gather x1, waiting for transfers between devices, local(): lax.all_gather(w_qkv, 'fsdp', axis=0, tiled=True)  99 us
    another operation x32, matrix products, span_factors(): jax.scipy.linalg.solve_triangular(system, right_side, lower=True, unit_di...  68.7 us
    dot_general x32, matrix products, span_output(): jnp.einsum('ist,itn->isn', query_rows, memory_matrix, precision=exact_pre...  68.5 us
    ppermute x2, waiting for transfers between devices, gather_around(): lax.ppermute(going_up, axis, [(d, (d + 1) % ways) for d in range(ways)])  65.4 us
    dot_general x32, matrix products, span_output(): jnp.einsum('ist,itn->isn', key_blend, memory_matrix, precision=exact_prec...  59.1 us
  transfers between devices with their start and end apart: 14, of which 6 were waited for; matrix products, arithmetic and copies ran while one was open for 63% of the time, Pallas kernels for 0%

profile of v1, /device:TPU:0, one launch (start us, length us, event | category | flops | bytes accessed | tf_op | source)
XLA Modules:
  0.0 2539.1 jit_solution(10155632397167235328)
XLA Ops:
  8.8 3.1 collective-permute-start
  14.7 117.1 %all_gather.19 = bf16[1024,8]{0,1:T(8,128)(2,1)S(1)} all-gather(bf16[256,8]{0,1:T(8,128)(2,1)S(1)} %copy-done.55), channel_id=1, replica_groups=mesh['dp'=4,'fsdp'=4,'ctx'=2] {'fsdp'}, dimensions={0}, use_global_device_ids=true | all-gather | bytes 20480 | tf_op jit(solution)/shard_map/all_gather | solution.py:144
  133.1 3.4 broadcast_in_dim.211
  145.3 65.4 %collective-permute-done.2 = bf16[256,3072]{1,0:T(8,128)(2,1)} collective-permute-done((bf16[256,3072]{1,0:T(8,128)(2,1)}, bf16[256,3072]{1,0:T(8,128)(2,1)}, u32[]{:S(2)}, u32[]{:S(2)}) %collective-permute-start.2) | collective-permute-done | bytes 1572896 | tf_op jit(solution)/shard_map/ppermute | solution.py:19
  213.4 5.7 convolution_multiply_fusion.1
  223.9 13.0 fusion.151
  244.3 413.5 %while.99 = (s32[]{:T(128)}, f32[8,128,128]{2,1,0:T(8,128)S(1)}, f32[8,128,128]{2,1,0:T(8,128)}, f32[8,8,64,128]{3,2,1,0:T(8,128)S(1)}, f32[8,8,64]{2,1,0:T(8,12...) while((s32[]{:T(128)}, f32[8,128,128]{2,1,0:T(8,128)S(1)}, ...), condition=%wide.region_3.5_spmd.clone, body=%wide.region_2.4_spmd.clone.sunk | while | flops 655380544 | bytes 13583016 | solution.py:176
  247.4 40.7 %custom-call.39 = f32[8,1,64,64]{2,3,1,0:T(8,128)} custom-call(f32[8,1,64,64]{3,2,1,0:T(8,128)} %fusion.417), custom_call_target="InvertDiagBlocksLowerTriangular" | custom-call | tf_op jit(solution)/shard_map/while/body/eval_jaxpr/jit(_solve_triangular)/vmap()/triangular_solve/custom-call.1 | solution.py:49
  299.0 40.7 %custom-call.39 = f32[8,1,64,64]{2,3,1,0:T(8,128)} custom-call(f32[8,1,64,64]{3,2,1,0:T(8,128)} %fusion.417), custom_call_target="InvertDiagBlocksLowerTriangular" | custom-call | tf_op jit(solution)/shard_map/while/body/eval_jaxpr/jit(_solve_triangular)/vmap()/triangular_solve/custom-call.1 | solution.py:49
  350.8 40.7 %custom-call.39 = f32[8,1,64,64]{2,3,1,0:T(8,128)} custom-call(f32[8,1,64,64]{3,2,1,0:T(8,128)} %fusion.417), custom_call_target="InvertDiagBlocksLowerTriangular" | custom-call | tf_op jit(solution)/shard_map/while/body/eval_jaxpr/jit(_solve_triangular)/vmap()/triangular_solve/custom-call.1 | solution.py:49
  402.5 40.7 %custom-call.39 = f32[8,1,64,64]{2,3,1,0:T(8,128)} custom-call(f32[8,1,64,64]{3,2,1,0:T(8,128)} %fusion.417), custom_call_target="InvertDiagBlocksLowerTriangular" | custom-call | tf_op jit(solution)/shard_map/while/body/eval_jaxpr/jit(_solve_triangular)/vmap()/triangular_solve/custom-call.1 | solution.py:49
  454.1 40.7 %custom-call.39 = f32[8,1,64,64]{2,3,1,0:T(8,128)} custom-call(f32[8,1,64,64]{3,2,1,0:T(8,128)} %fusion.417), custom_call_target="InvertDiagBlocksLowerTriangular" | custom-call | tf_op jit(solution)/shard_map/while/body/eval_jaxpr/jit(_solve_triangular)/vmap()/triangular_solve/custom-call.1 | solution.py:49
  505.8 40.7 %custom-call.39 = f32[8,1,64,64]{2,3,1,0:T(8,128)} custom-call(f32[8,1,64,64]{3,2,1,0:T(8,128)} %fusion.417), custom_call_target="InvertDiagBlocksLowerTriangular" | custom-call | tf_op jit(solution)/shard_map/while/body/eval_jaxpr/jit(_solve_triangular)/vmap()/triangular_solve/custom-call.1 | solution.py:49
  557.5 40.7 %custom-call.39 = f32[8,1,64,64]{2,3,1,0:T(8,128)} custom-call(f32[8,1,64,64]{3,2,1,0:T(8,128)} %fusion.417), custom_call_target="InvertDiagBlocksLowerTriangular" | custom-call | tf_op jit(solution)/shard_map/while/body/eval_jaxpr/jit(_solve_triangular)/vmap()/triangular_solve/custom-call.1 | solution.py:49
  609.2 40.7 %custom-call.39 = f32[8,1,64,64]{2,3,1,0:T(8,128)} custom-call(f32[8,1,64,64]{3,2,1,0:T(8,128)} %fusion.417), custom_call_target="InvertDiagBlocksLowerTriangular" | custom-call | tf_op jit(solution)/shard_map/while/body/eval_jaxpr/jit(_solve_triangular)/vmap()/triangular_solve/custom-call.1 | solution.py:49
  668.1 469.9 %while.97 = (s32[]{:T(128)}, f32[8,128,128]{2,1,0:T(8,128)S(1)}, f32[8,8,64,128]{3,2,0,1:T(8,128)}, f32[8,8,64,1]{2,1,3,0:T(8,128)S(1)}, f32[8,8,64,64]{3,2,1,0:...) while((s32[]{:T(128)}, f32[8,128,128]{2,1,0:T(8,128)S(1)}, ...), condition=%wide.region_6.8_spmd.clone, body=%wide.region_5.7_spmd.clone.sunk | while | flops 554618944 | bytes 16134973 | solution.py:108
  675.1 40.7 %custom-call.37 = f32[8,1,64,64]{2,3,1,0:T(8,128)} custom-call(f32[8,1,64,64]{3,2,1,0:T(8,128)} %add_bitcast_fusion.4), custom_call_target="InvertDiagBlocksLowerTriangular" | custom-call | tf_op jit(solution)/shard_map/jvp()/while/body/eval_jaxpr/jit(_solve_triangular)/vmap()/triangular_solve/custom-call.1 | solution.py:49
  733.8 40.7 %custom-call.37 = f32[8,1,64,64]{2,3,1,0:T(8,128)} custom-call(f32[8,1,64,64]{3,2,1,0:T(8,128)} %add_bitcast_fusion.4), custom_call_target="InvertDiagBlocksLowerTriangular" | custom-call | tf_op jit(solution)/shard_map/jvp()/while/body/eval_jaxpr/jit(_solve_triangular)/vmap()/triangular_solve/custom-call.1 | solution.py:49
  792.5 40.7 %custom-call.37 = f32[8,1,64,64]{2,3,1,0:T(8,128)} custom-call(f32[8,1,64,64]{3,2,1,0:T(8,128)} %add_bitcast_fusion.4), custom_call_target="InvertDiagBlocksLowerTriangular" | custom-call | tf_op jit(solution)/shard_map/jvp()/while/body/eval_jaxpr/jit(_solve_triangular)/vmap()/triangular_solve/custom-call.1 | solution.py:49
  851.4 40.7 %custom-call.37 = f32[8,1,64,64]{2,3,1,0:T(8,128)} custom-call(f32[8,1,64,64]{3,2,1,0:T(8,128)} %add_bitcast_fusion.4), custom_call_target="InvertDiagBlocksLowerTriangular" | custom-call | tf_op jit(solution)/shard_map/jvp()/while/body/eval_jaxpr/jit(_solve_triangular)/vmap()/triangular_solve/custom-call.1 | solution.py:49
  910.1 40.7 %custom-call.37 = f32[8,1,64,64]{2,3,1,0:T(8,128)} custom-call(f32[8,1,64,64]{3,2,1,0:T(8,128)} %add_bitcast_fusion.4), custom_call_target="InvertDiagBlocksLowerTriangular" | custom-call | tf_op jit(solution)/shard_map/jvp()/while/body/eval_jaxpr/jit(_solve_triangular)/vmap()/triangular_solve/custom-call.1 | solution.py:49
  968.8 40.7 %custom-call.37 = f32[8,1,64,64]{2,3,1,0:T(8,128)} custom-call(f32[8,1,64,64]{3,2,1,0:T(8,128)} %add_bitcast_fusion.4), custom_call_target="InvertDiagBlocksLowerTriangular" | custom-call | tf_op jit(solution)/shard_map/jvp()/while/body/eval_jaxpr/jit(_solve_triangular)/vmap()/triangular_solve/custom-call.1 | solution.py:49
  1027.5 40.7 %custom-call.37 = f32[8,1,64,64]{2,3,1,0:T(8,128)} custom-call(f32[8,1,64,64]{3,2,1,0:T(8,128)} %add_bitcast_fusion.4), custom_call_target="InvertDiagBlocksLowerTriangular" | custom-call | tf_op jit(solution)/shard_map/jvp()/while/body/eval_jaxpr/jit(_solve_triangular)/vmap()/triangular_solve/custom-call.1 | solution.py:49
  1086.3 40.7 %custom-call.37 = f32[8,1,64,64]{2,3,1,0:T(8,128)} custom-call(f32[8,1,64,64]{3,2,1,0:T(8,128)} %add_bitcast_fusion.4), custom_call_target="InvertDiagBlocksLowerTriangular" | custom-call | tf_op jit(solution)/shard_map/jvp()/while/body/eval_jaxpr/jit(_solve_triangular)/vmap()/triangular_solve/custom-call.1 | solution.py:49
  1145.3 4.8 multiply_reduce_fusion.6
  1150.1 12.2 fusion.218
  1162.3 11.6 multiply_convert_fusion.1
  1176.5 11.1 fusion.152
  1187.6 13.4 multiply_reduce_fusion.4
  1210.8 48.9 %while.100 = (s32[]{:T(128)}, f32[8,128,128]{2,1,0:T(8,128)S(1)}, f32[8,8,64,128]{3,2,1,0:T(8,128)}, f32[8,8,64,128]{3,2,1,0:T(8,128)}, f32[8,8,64,128]{3,2,1,0:...) while((s32[]{:T(128)}, f32[8,128,128]{2,1,0:T(8,128)S(1)}, ...), condition=%wide.region_12.14_spmd.clone, body=%wide.region_11.13_spmd.clone.sunk | while | flops 352976896 | bytes 5245579 | solution.py:108
  1262.0 9.6 fusion.204
  1272.9 4.8 fusion.201
  1283.5 541.7 %while.98 = (s32[]{:T(128)}, f32[8,128,128]{2,1,0:T(8,128)S(1)}, f32[8,8,64,128]{3,2,0,1:T(8,128)}, f32[8,8,64,128]{3,2,0,1:T(8,128)}, f32[8,8,64,128]{3,2,0,1:T...) while((s32[]{:T(128)}, f32[8,128,128]{2,1,0:T(8,128)S(1)}, ...), condition=%wide.region_16.18_spmd.clone.clone, body=%wide.region_13.17_spmd.clone.clone.sunk | while | flops 1134243328 | bytes 18174760 | solution.py:108
  1283.7 2.8 fusion.396
  1301.4 40.7 %custom-call.38 = f32[8,1,64,64]{2,3,1,0:T(8,128)} custom-call(f32[8,1,64,64]{3,2,1,0:T(8,128)} %add_bitcast_fusion.5), custom_call_target="InvertDiagBlocksLowerTriangular" | custom-call | tf_op jit(solution)/shard_map/transpose(jvp())/while/body/eval_jaxpr/jit(_solve_triangular)/vmap()/triangular_solve | solution.py:49
  1351.4 2.8 fusion.396
  1369.1 40.7 %custom-call.38 = f32[8,1,64,64]{2,3,1,0:T(8,128)} custom-call(f32[8,1,64,64]{3,2,1,0:T(8,128)} %add_bitcast_fusion.5), custom_call_target="InvertDiagBlocksLowerTriangular" | custom-call | tf_op jit(solution)/shard_map/transpose(jvp())/while/body/eval_jaxpr/jit(_solve_triangular)/vmap()/triangular_solve | solution.py:49
  1419.1 2.8 fusion.396
  1436.8 40.7 %custom-call.38 = f32[8,1,64,64]{2,3,1,0:T(8,128)} custom-call(f32[8,1,64,64]{3,2,1,0:T(8,128)} %add_bitcast_fusion.5), custom_call_target="InvertDiagBlocksLowerTriangular" | custom-call | tf_op jit(solution)/shard_map/transpose(jvp())/while/body/eval_jaxpr/jit(_solve_triangular)/vmap()/triangular_solve | solution.py:49
  1486.9 2.8 fusion.396
  1504.5 40.7 %custom-call.38 = f32[8,1,64,64]{2,3,1,0:T(8,128)} custom-call(f32[8,1,64,64]{3,2,1,0:T(8,128)} %add_bitcast_fusion.5), custom_call_target="InvertDiagBlocksLowerTriangular" | custom-call | tf_op jit(solution)/shard_map/transpose(jvp())/while/body/eval_jaxpr/jit(_solve_triangular)/vmap()/triangular_solve | solution.py:49
  1554.5 2.8 fusion.396
  1572.2 40.7 %custom-call.38 = f32[8,1,64,64]{2,3,1,0:T(8,128)} custom-call(f32[8,1,64,64]{3,2,1,0:T(8,128)} %add_bitcast_fusion.5), custom_call_target="InvertDiagBlocksLowerTriangular" | custom-call | tf_op jit(solution)/shard_map/transpose(jvp())/while/body/eval_jaxpr/jit(_solve_triangular)/vmap()/triangular_solve | solution.py:49
  1622.2 2.8 fusion.396
  1639.8 40.7 %custom-call.38 = f32[8,1,64,64]{2,3,1,0:T(8,128)} custom-call(f32[8,1,64,64]{3,2,1,0:T(8,128)} %add_bitcast_fusion.5), custom_call_target="InvertDiagBlocksLowerTriangular" | custom-call | tf_op jit(solution)/shard_map/transpose(jvp())/while/body/eval_jaxpr/jit(_solve_triangular)/vmap()/triangular_solve | solution.py:49
  1689.9 2.8 fusion.396
  1707.5 40.7 %custom-call.38 = f32[8,1,64,64]{2,3,1,0:T(8,128)} custom-call(f32[8,1,64,64]{3,2,1,0:T(8,128)} %add_bitcast_fusion.5), custom_call_target="InvertDiagBlocksLowerTriangular" | custom-call | tf_op jit(solution)/shard_map/transpose(jvp())/while/body/eval_jaxpr/jit(_solve_triangular)/vmap()/triangular_solve | solution.py:49
  1757.6 2.8 fusion.396
  1775.2 40.7 %custom-call.38 = f32[8,1,64,64]{2,3,1,0:T(8,128)} custom-call(f32[8,1,64,64]{3,2,1,0:T(8,128)} %add_bitcast_fusion.5), custom_call_target="InvertDiagBlocksLowerTriangular" | custom-call | tf_op jit(solution)/shard_map/transpose(jvp())/while/body/eval_jaxpr/jit(_solve_triangular)/vmap()/triangular_solve | solution.py:49
  1828.2 2.8 fusion.167
  1838.3 5.7 multiply_reduce_fusion.3
  1844.1 5.4 broadcast_multiply_fusion.4
  1849.5 6.3 pad_add_fusion.3
  1859.6 6.7 fusion.221
  1866.3 26.1 %pad_maximum_fusion.2 = f32[1024,9736]{1,0:T(8,128)} fusion(f32[1024,8]{1,0:T(8,128)S(1)} %fusion.219, f32[1024,5632]{1,0:T(8,128)} %fusion.152, f32[1024,1024]{1,0:T(8,128)S(1)} %copy-done.10, f32[1024,3072]{1,0:T(8,128)} %fusion.221), kind=kLoop, calls=%fused_computation.201 | loop fusion | flops 29908992 | bytes 79757312 | tf_op jit(solution)/shard_map/concatenate | solution.py:330
  1895.7 421.4 %reduce-scatter.3.cloned.1.call-done = f32[128,9736]{1,0:T(8,128)} async-done(((f32[1024,9736]{1,0:T(8,128)}), f32[128,9736]{1,0:T(8,128)}) %reduce-scatter.3.cloned.1.call-update) | async-done | bytes 4984848 | tf_op jit(solution)/shard_map/reduce_scatter | solution.py:329
  2317.1 4.2 convert_element_type.180
  2322.8 8.6 fusion.194
  2333.3 99.0 %all-gather.11.cloned.1.call-done = bf16[1024,3072]{1,0:T(8,128)(2,1)} async-done(((bf16[256,3072]{1,0:T(8,128)(2,1)}), bf16[1024,3072]{1,0:T(8,128)(2,1)}) %all-gather.11.cloned.1.call-update) | async-done | bytes 6291472 | tf_op jit(solution)/shard_map/all_gather | solution.py:207
  2432.3 10.4 fusion.162
  2442.7 26.4 %all-reduce.7 = (bf16[1024]{0:T(1024)(128)(2,1)S(1)}, bf16[4,3072]{1,0:T(4,128)(2,1)S(1)}, bf16[128]{0:T(256)(128)(2,1)S(1)}, bf16[1024]{0:T(1024)(128)(2,1)S(1)}) all-reduce(f32[1024]{0:T(1024)S(1)} %get-tuple-element.1318, f32[4,3072]{1,0:T(4,128)S(1)} %pad_maximum_fusion.7, ...), channel_id=1, replica_groups=mesh['dp'=4,'fsdp'=4,'ctx'=2] {'fsdp','ctx'}, use_global_device_ids=true, to_apply=%region_21.23 | all-reduce | flops 14464 | bytes 86784 | tf_op jit(solution)/shard_map/psum | solution.py:338
  2469.1 16.7 all-reduce.8
  2488.1 3.2 fusion.200
  2491.3 33.5 %all-reduce.12.cloned.1.call-done = (bf16[128,9736]{1,0:T(8,128)(2,1)}, bf16[352,1024]{1,0:T(8,128)(2,1)}) async-done(((bf16[128,9736]{1,0:T(8,128)(2,1)}, bf16[352,1024]{1,0:T(8,128)(2,1)}), (bf16[128,9736]{1,0:T(8,128)(2,1)}, bf16[352,1024]{1,0:T(8,128)(2,1)})) %all-reduce.12.cloned.1.call-update) | async-done | bytes 3213328 | tf_op jit(solution)/shard_map/psum | solution.py:342
  (776 shorter events, 570.1 us)
Async XLA Ops:
  7.2 1138.1 %all-gather.5.cloned.1.call-start = ((), (), s32[]{:S(2)}) async-start(), calls=%async_computation.2 | async-start | bytes 2621440 | tf_op jit(solution)/shard_map/all_gather | solution.py:145
  7.9 6.7 copy-start.55
  7.9 123.8 %copy-start.22 = (bf16[1,512,1024]{2,1,0:T(8,128)(2,1)S(1)}, bf16[1,512,1024]{2,1,0:T(8,128)(2,1)}, u32[]{:S(2)}) copy-start(bf16[1,512,1024]{2,1,0:T(8,128)(2,1)} %param.22) | copy-start | bytes 3145732
  7.9 124.7 %copy-start.56 = (f32[1024]{0:T(1024)S(1)}, f32[1024]{0:T(1024)}, u32[]{:S(2)}) copy-start(f32[1024]{0:T(1024)} %param.25) | copy-start | bytes 12292
  8.0 1142.1 %all-gather.7.cloned.1.call-start = ((), (), s32[]{:S(2)}) async-start(), calls=%async_computation.3 | async-start | bytes 14417920 | tf_op jit(solution)/shard_map/all_gather | solution.py:148
  8.7 1153.6 %all-gather.9.cloned.1.call-start = ((), (), s32[]{:S(2)}) async-start(), calls=%async_computation.4 | async-start | bytes 7208960 | tf_op jit(solution)/shard_map/all_gather | solution.py:149
  8.8 129.1 %collective-permute-start = (bf16[256,3072]{1,0:T(8,128)(2,1)S(1)}, bf16[256,3072]{1,0:T(8,128)(2,1)}, u32[]{:S(2)}, u32[]{:S(2)}) collective-permute-start(bf16[256,3072]{1,0:T(8,128)(2,1)S(1)} %copy-done.25), channel_id=1, source_target_pairs={{0,2},{2,4},{4,6},{6,0},{1,3},{3,5},{5,7},{7,1},{8,10},{10,12},{12... | collective-permute-start | bytes 4718600 | tf_op jit(solution)/shard_map/ppermute | solution.py:19
  11.8 130.8 %collective-permute-start.1 = (bf16[256,3072]{1,0:T(8,128)(2,1)S(1)}, bf16[256,3072]{1,0:T(8,128)(2,1)}, u32[]{:S(2)}, u32[]{:S(2)}) collective-permute-start(bf16[256,3072]{1,0:T(8,128)(2,1)S(1)} %copy-done.25), channel_id=1, source_target_pairs={{0,6},{2,0},{4,2},{6,4},{1,7},{3,1},{5,3},{7,5},{8,14},{10,8},{12,... | collective-permute-start | bytes 4718600 | tf_op jit(solution)/shard_map/ppermute | solution.py:22
  14.0 1879.4 %reduce-scatter.5.cloned.1.call-start = ((), (), s32[]{:S(2)}) async-start(), calls=%async_computation.7 | async-start | bytes 12976128 | tf_op jit(solution)/shard_map/reduce_scatter | solution.py:332
  132.6 80.8 %copy-start.51 = (f32[512]{0:T(512)}, f32[512]{0:T(512)S(1)}, u32[]{:S(2)}) copy-start(f32[512]{0:T(512)S(1)} %get-tuple-element.1475) | copy-start | bytes 6148
  133.1 4.7 copy-start.47
  137.8 72.9 %collective-permute-start.2 = (bf16[256,3072]{1,0:T(8,128)(2,1)}, bf16[256,3072]{1,0:T(8,128)(2,1)}, u32[]{:S(2)}, u32[]{:S(2)}) collective-permute-start(bf16[256,3072]{1,0:T(8,128)(2,1)} %collective-permute-done), channel_id=1, source_target_pairs={{0,2},{2,4},{4,6},{6,0},{1,3},{3,5},{5,7},{7,1},{8,10},{10,12},{12... | collective-permute-start | bytes 4718600 | tf_op jit(solution)/shard_map/ppermute | solution.py:19
  139.9 84.0 %copy-start.36 = (f32[1,3072]{1,0:T(1,128)}, f32[1,3072]{1,0:T(1,128)S(1)}, u32[]{:S(2)}) copy-start(f32[1,3072]{1,0:T(1,128)S(1)} %get-tuple-element.1466) | copy-start | bytes 36868
  139.9 84.0 %copy-start.38 = (f32[1,3072]{1,0:T(1,128)}, f32[1,3072]{1,0:T(1,128)S(1)}, u32[]{:S(2)}) copy-start(f32[1,3072]{1,0:T(1,128)S(1)} %get-tuple-element.1467) | copy-start | bytes 36868
  139.9 84.0 %copy-start.40 = (f32[1,3072]{1,0:T(1,128)}, f32[1,3072]{1,0:T(1,128)S(1)}, u32[]{:S(2)}) copy-start(f32[1,3072]{1,0:T(1,128)S(1)} %get-tuple-element.1468) | copy-start | bytes 36868
  139.9 84.0 %copy-start.42 = (f32[1,3072]{1,0:T(1,128)}, f32[1,3072]{1,0:T(1,128)S(1)}, u32[]{:S(2)}) copy-start(f32[1,3072]{1,0:T(1,128)S(1)} %get-tuple-element.1469) | copy-start | bytes 36868
  221.7 2.1 collective-permute-start.3
  223.8 13.0 copy-start.31
  342.3 3.9 copy-start.8
  657.8 6.4 copy-start.4
  659.5 6.7 collective-permute-start.4
  718.4 5.0 copy-start.1
  777.1 3.9 copy-start.11
  777.1 5.0 copy-start.1
  835.8 5.0 copy-start.1
  894.7 3.9 copy-start.11
  894.7 5.0 copy-start.1
  953.4 5.0 copy-start.1
  1012.1 5.0 copy-start.1
  1070.8 3.9 copy-start.11
  1070.8 5.0 copy-start.1
  1129.6 3.9 copy-start.11
  1129.6 5.0 copy-start.1
  1145.3 4.8 copy-start.33
  1162.3 14.2 copy-start.16
  1187.6 13.4 copy-start.29
  1210.8 48.9 %copy-start.9 = (f32[8,128,128]{2,1,0:T(8,128)S(1)}, f32[8,128,128]{2,1,0:T(8,128)}, u32[]{:S(2)}) copy-start(f32[8,128,128]{2,1,0:T(8,128)} %get-tuple-element.962) | copy-start | bytes 1572868
  1260.7 16.9 collective-permute-start.5
  1271.7 1045.4 %reduce-scatter.3.cloned.1.call-start = ((), (), s32[]{:S(2)}) async-start(), calls=%async_computation.6 | async-start | bytes 45416448 | tf_op jit(solution)/shard_map/reduce_scatter | solution.py:329
  1342.1 5.2 copy-start.12
  1409.8 5.2 copy-start.12
  1477.5 5.2 copy-start.12
  1545.2 5.2 copy-start.12
  1612.9 5.2 copy-start.12
  1680.5 5.2 copy-start.12
  1748.2 5.2 copy-start.12
  1815.9 5.2 copy-start.12
  1831.1 6.1 slice-start.2
  1838.2 5.8 copy-start.37
  1838.2 5.8 copy-start.39
  1838.3 5.8 copy-start.41
  1838.3 5.8 copy-start.43
  1849.5 7.6 copy-start.48
  1849.5 7.7 copy-start.23
  1849.5 7.7 copy-start.52
  1849.5 7.7 copy-start.57
  1855.8 3.7 collective-permute-start.6
  1859.6 6.7 copy-start.10
  1892.4 539.9 %all-gather.11.cloned.1.call-start = ((), (), s32[]{:S(2)}) async-start(), calls=%async_computation.5 | async-start | bytes 7864320 | tf_op jit(solution)/shard_map/all_gather | solution.py:207
  1893.0 631.7 %all-reduce.12.cloned.1.call-start = ((), (), s32[]{:S(2)}) async-start(), calls=%async_computation.8 | async-start | bytes 6488064 | tf_op jit(solution)/shard_map/psum | solution.py:342
  2322.8 8.6 copy-start.46
  2333.3 109.4 %copy-start.54 = (f32[1024]{0:T(1024)S(1)}, f32[1024]{0:T(1024)}, u32[]{:S(2)}) copy-start(f32[1024]{0:T(1024)} %get-tuple-element.1314) | copy-start | bytes 12292
  2333.3 154.8 %copy-start.15 = (f32[512,1024]{1,0:T(8,128)S(1)}, f32[512,1024]{1,0:T(8,128)}, u32[]{:S(2)}) copy-start(f32[512,1024]{1,0:T(8,128)} %copy-done.14) | copy-start | bytes 6291460
  2333.3 154.8 %copy-start.50 = (f32[512]{0:T(512)S(1)}, f32[512]{0:T(512)}, u32[]{:S(2)}) copy-start(f32[512]{0:T(512)} %get-tuple-element.1474) | copy-start | bytes 6148
  (54 other events, 139.4 us)
Sparse Core Ops, SparseCore 0:
  9.6 89.7 all-gather.4
  100.9 234.7 all-gather.6
  337.3 106.1 all-gather.8
  1271.8 155.4 reduce-scatter.4
  1892.5 424.4 reduce-scatter.2
  2318.6 113.7 all-gather.10
  2436.4 88.2 all-reduce.11
